TPU v7x, 512 devices: a whole 4x4x16 slice. The times are simulated.
512 devices in a mesh: rows: 64 (over z, y), cls: 8 (over x, core).
Axes of the slice: x: 4, y: 4, z: 16, core: 2. Of those that a mesh axis runs over, the one named last changes fastest.
Arguments:
- logits: float32 [262144, 1024], P('rows', 'cls'), may hold values from -24 to 360, as said below
- leaf_index: int32 [262144], P('rows'), may hold values from 0 to 127
- labels: int32 [262144], P('rows'), may hold values from 0 to 1023
Outputs:
- leaf_values: float32 [128, 1024], P(None, 'cls')
- updated: float32 [262144, 1024], P('rows', 'cls')
Inputs may be any that keep to these rules, and one draw needn't show every extreme that they name: `logits`: raw scores of a model in training.
All inputs are finite; a program needn't handle non-finite values.
Results may differ from a plain program's by a relative error of at most 0.0003.
Values sent between devices are 32-bit elements; how exact they have to be, the bound alone decides.
A program may use at most 64 MiB of HBM per device.

v0:
```python
import jax
import jax.numpy as jnp
from jax import lax
from jax.sharding import PartitionSpec as P

LEAVES = 128


def per_device(logits, leaf_index, labels):
    row_count, class_width = logits.shape
    peak = lax.pmax(jnp.max(logits, axis=1, keepdims=True), "cls")
    expo = jnp.exp(logits - peak)
    total = lax.psum(jnp.sum(expo, axis=1, keepdims=True), "cls")
    prob = expo / total
    offset = lax.axis_index("cls") * class_width
    classes = offset + jnp.arange(class_width, dtype=jnp.int32)[None, :]
    grad = prob - (labels[:, None] == classes).astype(jnp.float32)
    hess = prob * (1.0 - prob)
    leaves = jnp.arange(LEAVES, dtype=jnp.int32)[None, :]
    onehot = (leaf_index[:, None] == leaves).astype(jnp.float32)
    dims = (((0,), (0,)), ((), ()))
    g_part = lax.dot_general(
        onehot, grad, dims, precision=lax.Precision.HIGHEST, preferred_element_type=jnp.float32
    )
    h_part = lax.dot_general(
        onehot, hess, dims, precision=lax.Precision.HIGHEST, preferred_element_type=jnp.float32
    )
    g_sum, h_sum = lax.psum((g_part, h_part), "rows")
    leaf_values = -0.3 * g_sum / (h_sum + 1.0)
    updated = logits + jnp.dot(
        onehot, leaf_values, precision=lax.Precision.HIGHEST, preferred_element_type=jnp.float32
    )
    return (leaf_values, updated)


def solution(mesh):
    return jax.shard_map(
        per_device,
        mesh=mesh,
        in_specs=(P("rows", "cls"), P("rows"), P("rows")),
        out_specs=(P(None, "cls"), P("rows", "cls")),
        check_vma=False,
    )
```

profile of v0, /device:TPU:2, one launch (start us, length us, event | category | flops | bytes accessed | tf_op | source)
XLA Modules:
  0.0 344.5 jit_solution(12549571589093608618)
XLA Ops:
  7.2 0.0 copy-start
  7.2 0.0 all-reduce.3.cloned.1.call-start
  7.2 2.3 reduce_max.9
  9.6 26.0 %pmax.7 = f32[4096]{0:T(1024)S(1)} all-reduce(f32[4096]{0:T(1024)S(1)} %reduce_max.9), channel_id=1, replica_groups=mesh['rows'=64,'cls'=8] {'cls'}, use_global_device_ids=true, to_apply=%region_1.0 | all-reduce | flops 4096 | bytes 32768 | tf_op jit(solution)/shard_map/pmax | solution.py:11
  35.6 0.0 copy-done
  35.6 1.3 fusion.6
  36.9 23.6 %psum.21 = f32[4096]{0:T(1024)S(1)} all-reduce(f32[4096]{0:T(1024)S(1)} %fusion.6), channel_id=1, replica_groups=mesh['rows'=64,'cls'=8] {'cls'}, use_global_device_ids=true, to_apply=%region_3.0 | all-reduce | flops 4096 | bytes 32768 | tf_op jit(solution)/shard_map/psum | solution.py:13
  60.4 0.0 copy-start.2
  60.4 2.3 fusion.5
  62.7 0.0 copy-done.2
  62.7 0.0 copy-start.3
  62.7 3.5 %fusion = f32[128,128]{1,0:T(8,128)} fusion(f32[4096,128]{1,0:T(8,128)S(1)} %fusion.5, s32[4096]{0:T(1024)S(1)} %copy-done.2), kind=kOutput, calls=%fused_computation.2 | convolution fusion | flops 806879232 | bytes 2179072 | tf_op jit(solution)/shard_map/dot_general | solution.py:25
  66.2 0.0 copy-done.3
  66.2 3.6 %fusion.1 = f32[128,128]{1,0:T(8,128)} fusion(f32[4096,128]{1,0:T(8,128)S(1)} %fusion.5, s32[128]{0:T(128)S(1)} %iota_add_fusion, s32[4096]{0:T(1024)S(1)} %copy-done.2, s32[4096]{0:T(1024)S(1)} %copy-done.3), kind=kOutput, calls=%fused_computation.3 | convolution fusion | flops 807403520 | bytes 2195968 | tf_op jit(solution)/shard_map/dot_general | solution.py:22
  69.8 0.0 all-reduce.3.cloned.1.call-update
  69.8 262.6 %all-reduce.3.cloned.1.call-done = (f32[128,128]{1,0:T(8,128)}, f32[128,128]{1,0:T(8,128)}) async-done(((f32[128,128]{1,0:T(8,128)}, f32[128,128]{1,0:T(8,128)}), (f32[128,128]{1,0:T(8,128)}, f32[128,128]{1,0:T(8,128)})) %all-reduce.3.cloned.1.call-update) | async-done | bytes 131088 | tf_op jit(solution)/shard_map/psum | solution.py:28
  332.5 0.9 add_divide_fusion
  333.4 0.0 copy-start.1
  333.4 4.2 %convolution_add_fusion = f32[4096,128]{1,0:T(8,128)} fusion(f32[4096,128]{1,0:T(8,128)S(1)} %copy-done, f32[128,128]{1,0:T(8,128)S(1)} %add_divide_fusion, s32[4096]{0:T(1024)S(1)} %copy-done.2), kind=kOutput, calls=%fused_computation | convolution fusion | flops 806354944 | bytes 4276224 | tf_op jit(solution)/shard_map/dot_general | solution.py:30
  337.6 0.0 copy-done.1
  (1 shorter events, 0.0 us)
Async XLA Ops:
  7.2 28.4 %copy-start = (f32[4096,128]{1,0:T(8,128)S(1)}, f32[4096,128]{1,0:T(8,128)}, u32[]{:S(2)}) copy-start(f32[4096,128]{1,0:T(8,128)} %param.3) | copy-start | bytes 6291460
  7.2 325.3 %all-reduce.3.cloned.1.call-start = ((), (), s32[]{:S(2)}) async-start(), calls=%async_computation | async-start | bytes 262144 | tf_op jit(solution)/shard_map/psum | solution.py:28
  60.4 2.3 copy-start.2
  62.7 3.5 %copy-start.3 = (s32[4096]{0:T(1024)S(1)}, s32[4096]{0:T(1024)}, u32[]{:S(2)}) copy-start(s32[4096]{0:T(1024)} %param.5) | copy-start | bytes 49156
  333.4 4.3 %copy-start.1 = (f32[128,128]{1,0:T(8,128)}, f32[128,128]{1,0:T(8,128)S(1)}, u32[]{:S(2)}) copy-start(f32[128,128]{1,0:T(8,128)S(1)} %add_divide_fusion) | copy-start | bytes 196612
Sparse Core Ops, SparseCore 0:
  69.9 262.4 all-reduce.2
where the time goes:
time: 345 us; the launch traced here: 344 us
  waiting for transfers between devices  263 us (76%)
  blocking collectives  49.6 us (14%)
  between operations  14.1 us (4%)
  matrix products  11.3 us (3%)
  other arithmetic  6.77 us (2%)
    psum x1, waiting for transfers between devices, per_device(): g_sum, h_sum = lax.psum((g_part, h_part), 'rows')  263 us
    pmax x1, blocking collectives, per_device(): peak = lax.pmax(jnp.max(logits, axis=1, keepdims=True), 'cls')  26 us
    psum x1, blocking collectives, per_device(): total = lax.psum(jnp.sum(expo, axis=1, keepdims=True), 'cls')  23.6 us
  transfers between devices with their start and end apart: 1, of which 1 were waited for; matrix products, arithmetic and copies ran while one was open for 0% of the time, Pallas kernels for 0%

commit v1 on v0

v1 whole, which is shorter than its diff:
```python
import functools

import jax
import jax.numpy as jnp
from jax import lax
from jax.experimental import pallas as pl
from jax.experimental.pallas import tpu as pltpu
from jax.sharding import PartitionSpec as P

LEAVES = 128
LANES = 128
MESH = pl.DeviceIdType.MESH
F32 = jnp.float32
BF16 = jnp.bfloat16
CHUNKS = 4


def split(value):
    high = value.astype(BF16)
    return high, (value - high.astype(F32)).astype(BF16)


def kernel(
    n_cls, n_y, n_z,
    x_hbm, leaf_ref, label_ref,
    lv_out, up_out,
    x_v, e_v, stats, onehot, terms, sums, y_in, z_out, z_in, lv_z, lv_y, lv_all,
    x_sem, up_sem, s_send, s_recv, yr_send, yr_recv, zr_send, zr_recv, za_send, za_recv, ya_send, ya_recv,
):
    row, cls = lax.axis_index("rows"), lax.axis_index("cls")
    z, y = row // n_y, row % n_y
    rows = x_v.shape[0]
    blocks = rows // LANES
    per_chunk = blocks // CHUNKS
    chunk_rows = rows // CHUNKS

    def cls_peer(d):
        return {"rows": row, "cls": lax.rem(cls + d, n_cls)}

    def y_peer(d):
        return {"rows": z * n_y + lax.rem(y + d, n_y), "cls": cls}

    def z_peer(d):
        return {"rows": lax.rem(z + d, n_z) * n_y + y, "cls": cls}

    loads = []
    for c in range(CHUNKS):
        part = pl.ds(c * chunk_rows, chunk_rows)
        load = pltpu.make_async_copy(x_hbm.at[part], x_v.at[part], x_sem.at[c])
        load.start()
        loads.append(load)

    barrier = pltpu.get_barrier_semaphore()
    for d in range(1, n_cls):
        pl.semaphore_signal(barrier, inc=1, device_id=cls_peer(d), device_id_type=MESH)
    for d in range(1, n_y):
        pl.semaphore_signal(barrier, inc=1, device_id=y_peer(d), device_id_type=MESH)
    for d in range(1, n_z):
        pl.semaphore_signal(barrier, inc=1, device_id=z_peer(d), device_id_type=MESH)

    exchanges = []
    for c in range(CHUNKS):
        loads[c].wait()

        def local(i, carry, c=c):
            at = pl.ds(pl.multiple_of((c * per_chunk + i) * LANES, LANES), LANES)
            xt = x_v[at, :].T
            peak = jnp.max(xt, axis=0, keepdims=True)
            expo = jnp.exp(xt - peak)
            e_v[:, at] = expo
            stats[0, c, 0, pl.ds(i, 1), :] = peak
            stats[0, c, 1, pl.ds(i, 1), :] = jnp.sum(expo, axis=0, keepdims=True)
            return carry

        lax.fori_loop(0, per_chunk, local, 0)
        if c == 0:
            pl.semaphore_wait(barrier, n_cls + n_y + n_z - 3)
        for d in range(1, n_cls):
            copy = pltpu.make_async_remote_copy(
                stats.at[0, c], stats.at[d, c], s_send.at[d, c], s_recv.at[d, c],
                device_id=cls_peer(d), device_id_type=MESH,
            )
            copy.start()
            exchanges.append(copy)

    def one_hot(i, carry):
        at = pl.ds(pl.multiple_of(i * LANES, LANES), LANES)
        which = lax.broadcasted_iota(jnp.int32, (LEAVES, LANES), 0)
        hot = (which == leaf_ref[pl.ds(i, 1), :]).astype(F32).T.astype(BF16)
        onehot[at, 0:LEAVES] = hot
        onehot[at, LEAVES : 2 * LEAVES] = hot
        return carry

    lax.fori_loop(0, blocks, one_hot, 0)

    width = e_v.shape[0]
    for c in range(CHUNKS):
        for d in range(1, n_cls):
            exchanges[c * (n_cls - 1) + d - 1].wait()
        peak = stats[0, c, 0]
        for d in range(1, n_cls):
            peak = jnp.maximum(peak, stats[d, c, 0])
        own = jnp.exp(stats[0, c, 0] - peak)
        total = stats[0, c, 1] * own
        for d in range(1, n_cls):
            total = total + stats[d, c, 1] * jnp.exp(stats[d, c, 0] - peak)
        stats[0, c, 1] = own / total

        def derive(i, carry, c=c):
            k = c * per_chunk + i
            at = pl.ds(pl.multiple_of(k * LANES, LANES), LANES)
            prob = e_v[:, at] * stats[0, c, 1, pl.ds(i, 1), :]
            classes = lax.broadcasted_iota(jnp.int32, (width, LANES), 0) + cls * width
            grad = prob - (classes == label_ref[pl.ds(k, 1), :]).astype(F32)
            hess = prob * (1.0 - prob)
            terms[0:width, at], terms[width : 2 * width, at] = split(grad)
            terms[2 * width : 3 * width, at], terms[3 * width : 4 * width, at] = split(hess)
            return carry

        lax.fori_loop(0, per_chunk, derive, 0)

    acc = jnp.dot(terms[...], onehot[:, 0:LEAVES], preferred_element_type=F32)
    sums[0] = acc[0:width] + acc[width : 2 * width]
    sums[1] = acc[2 * width : 3 * width] + acc[3 * width : 4 * width]

    quarter = width // n_y
    copies = []
    for d in range(1, n_y):
        theirs = pl.ds(pl.multiple_of(lax.rem(y + d, n_y) * quarter, quarter), quarter)
        copy = pltpu.make_async_remote_copy(
            sums.at[:, theirs], y_in.at[d - 1], yr_send.at[d], yr_recv.at[d],
            device_id=y_peer(d), device_id_type=MESH,
        )
        copy.start()
        copies.append(copy)
    mine = sums[:, pl.ds(pl.multiple_of(y * quarter, quarter), quarter), :]
    for d in range(1, n_y):
        copies[d - 1].wait()
        mine = mine + y_in[d - 1]

    few = quarter // n_z
    for k in range(n_z):
        z_out[k, 0] = mine[0, k * few : (k + 1) * few]
        z_out[k, 1] = mine[1, k * few : (k + 1) * few]
    copies = []
    for d in range(1, n_z):
        copy = pltpu.make_async_remote_copy(
            z_out.at[lax.rem(z + d, n_z)], z_in.at[d - 1], zr_send.at[d], zr_recv.at[d],
            device_id=z_peer(d), device_id_type=MESH,
        )
        copy.start()
        copies.append(copy)
    mine = z_out[z]
    for d in range(1, n_z):
        copies[d - 1].wait()
        mine = mine + z_in[d - 1]
    lv_z[z] = -0.3 * mine[0] / (mine[1] + 1.0)

    sends = []
    for d in range(1, n_z):
        copy = pltpu.make_async_remote_copy(
            lv_z.at[z], lv_z.at[z], za_send.at[d], za_recv.at[d],
            device_id=z_peer(d), device_id_type=MESH,
        )
        copy.start()
        sends.append(copy)
    for d in range(1, n_z):
        source = lax.rem(z + n_z - d, n_z)
        pltpu.make_async_remote_copy(
            lv_z.at[source], lv_z.at[source], za_send.at[d], za_recv.at[d],
            device_id=z_peer(d), device_id_type=MESH,
        ).wait_recv()
    for k in range(n_z):
        lv_y[y, k * few : (k + 1) * few] = lv_z[k]
    for d in range(1, n_y):
        copy = pltpu.make_async_remote_copy(
            lv_y.at[y], lv_y.at[y], ya_send.at[d], ya_recv.at[d],
            device_id=y_peer(d), device_id_type=MESH,
        )
        copy.start()
        sends.append(copy)
    for d in range(1, n_y):
        source = lax.rem(y + n_y - d, n_y)
        pltpu.make_async_remote_copy(
            lv_y.at[source], lv_y.at[source], ya_send.at[d], ya_recv.at[d],
            device_id=y_peer(d), device_id_type=MESH,
        ).wait_recv()

    leaf_values = lv_y[...].reshape(width, LEAVES).T
    lv_out[...] = leaf_values
    lv_all[0:LEAVES, :], lv_all[LEAVES : 2 * LEAVES, :] = split(leaf_values)

    def update(i, carry):
        at = pl.ds(pl.multiple_of(i * 256, 256), 256)
        up_out[at, :] = x_v[at, :] + jnp.dot(onehot[at, :], lv_all[...], preferred_element_type=F32)
        return carry

    lax.fori_loop(0, rows // 256, update, 0)
    for copy in sends:
        copy.wait_send()


def solution(mesh):
    n_cls, n_rows = mesh.shape["cls"], mesh.shape["rows"]
    n_y = 4
    n_z = n_rows // n_y

    def per_device(logits, leaf_index, labels):
        rows, width = logits.shape
        blocks = rows // LANES
        quarter = width // n_y
        few = quarter // n_z
        dma = pltpu.SemaphoreType.DMA
        vmem = pl.BlockSpec(memory_space=pltpu.VMEM)
        return pl.pallas_call(
            functools.partial(kernel, n_cls, n_y, n_z),
            out_shape=(
                jax.ShapeDtypeStruct((LEAVES, width), F32),
                jax.ShapeDtypeStruct((rows, width), F32),
            ),
            in_specs=[pl.BlockSpec(memory_space=pltpu.HBM), vmem, vmem],
            out_specs=(vmem, vmem),
            scratch_shapes=[
                pltpu.VMEM((rows, width), F32),
                pltpu.VMEM((width, rows), F32),
                pltpu.VMEM((n_cls, CHUNKS, 2, blocks // CHUNKS, LANES), F32),
                pltpu.VMEM((rows, 2 * LEAVES), BF16),
                pltpu.VMEM((4 * width, rows), BF16),
                pltpu.VMEM((2, width, LEAVES), F32),
                pltpu.VMEM((n_y - 1, 2, quarter, LEAVES), F32),
                pltpu.VMEM((n_z, 2, few, LEAVES), F32),
                pltpu.VMEM((n_z - 1, 2, few, LEAVES), F32),
                pltpu.VMEM((n_z, few, LEAVES), F32),
                pltpu.VMEM((n_y, quarter, LEAVES), F32),
                pltpu.VMEM((2 * LEAVES, width), BF16),
                dma((CHUNKS,)),
                dma((CHUNKS,)),
                dma((n_cls, CHUNKS)),
                dma((n_cls, CHUNKS)),
                dma((n_y,)),
                dma((n_y,)),
                dma((n_z,)),
                dma((n_z,)),
                dma((n_z,)),
                dma((n_z,)),
                dma((n_y,)),
                dma((n_y,)),
            ],
            compiler_params=pltpu.CompilerParams(
                collective_id=0, has_side_effects=True, vmem_limit_bytes=32 * 2**20
            ),
        )(logits, leaf_index.reshape(blocks, LANES), labels.reshape(blocks, LANES))

    return jax.shard_map(
        per_device,
        mesh=mesh,
        in_specs=(P("rows", "cls"), P("rows"), P("rows")),
        out_specs=(P(None, "cls"), P("rows", "cls")),
        check_vma=False,
    )
```

time: 345 us -> 57.9 us (0.17)
  the two profiles are of different devices: /device:TPU:2 before, /device:TPU:6 now
where the time goes in v1:
time: 57.9 us; the launch traced here: 57.6 us
  Pallas kernels  52 us (90%)
  local copies, waits for them, and re-layouts  4.97 us (9%)
  between operations  0.65 us (1%)
    pallas_call x1, Pallas kernels, per_device(): pl.pallas_call(functools.partial(kernel, n_cls, n_y, n_z), out_shape=(jax...  52 us
    unnamed x8, local copies, waits for them, and re-layouts  4.97 us

profile of v1, /device:TPU:6, one launch (start us, length us, event | category | flops | bytes accessed | tf_op | source)
XLA Modules:
  0.0 57.6 jit_solution(1722829047020571596)
XLA Ops:
  0.6 0.0 copy-start
  0.6 1.6 %copy-done = f32[4096,128]{1,0:T(8,128)S(1)} copy-done((f32[4096,128]{1,0:T(8,128)S(1)}, f32[4096,128]{1,0:T(8,128)}, u32[]{:S(2)}) %copy-start) | copy-done | bytes 2097176
  2.2 0.0 copy-start.1
  2.2 0.7 %copy-done.1 = s32[4096]{0:T(1024)S(1)} copy-done((s32[4096]{0:T(1024)S(1)}, s32[4096]{0:T(1024)}, u32[]{:S(2)}) %copy-start.1) | copy-done | bytes 16408
  2.9 0.0 copy-start.2
  2.9 0.7 %copy-done.2 = s32[4096]{0:T(1024)S(1)} copy-done((s32[4096]{0:T(1024)S(1)}, s32[4096]{0:T(1024)}, u32[]{:S(2)}) %copy-start.2) | copy-done | bytes 16408
  3.7 52.0 %shard_map.50 = (f32[128,128]{1,0:T(8,128)S(1)}, f32[4096,128]{1,0:T(8,128)S(1)}) custom-call(f32[4096,128]{1,0:T(8,128)S(1)} %copy-done, s32[32,128]{1,0:T(8,128)S(1)} %bitcast.2, s32[32,128]{1,0:T(8,128)S(1)} %bitcast.3), custom_call_target="tpu_custom_call" | custom-call | tf_op jit(solution)/shard_map/pallas_call | solution.py:215
  55.6 0.6 %copy.7 = f32[128,128]{1,0:T(8,128)} copy(f32[128,128]{1,0:T(8,128)S(1)} %get-tuple-element.4) | data formatting | bytes 131072
  56.3 1.3 %copy.8 = f32[4096,128]{1,0:T(8,128)} copy(f32[4096,128]{1,0:T(8,128)S(1)} %get-tuple-element.5) | data formatting | bytes 4194304
Async XLA Ops:
  0.6 1.6 %copy-start = (f32[4096,128]{1,0:T(8,128)S(1)}, f32[4096,128]{1,0:T(8,128)}, u32[]{:S(2)}) copy-start(f32[4096,128]{1,0:T(8,128)} %x_hbm.1) | copy-start | bytes 6291460
  2.2 0.7 %copy-start.1 = (s32[4096]{0:T(1024)S(1)}, s32[4096]{0:T(1024)}, u32[]{:S(2)}) copy-start(s32[4096]{0:T(1024)} %param.4) | copy-start | bytes 49156
  2.9 0.7 %copy-start.2 = (s32[4096]{0:T(1024)S(1)}, s32[4096]{0:T(1024)}, u32[]{:S(2)}) copy-start(s32[4096]{0:T(1024)} %param.5) | copy-start | bytes 49156

commit v2 on v1

v2 whole, which is shorter than its diff:
```python
import functools

import jax
import jax.numpy as jnp
from jax import lax
from jax.experimental import pallas as pl
from jax.experimental.pallas import tpu as pltpu
from jax.sharding import PartitionSpec as P

LEAVES = 128
LANES = 128
MESH = pl.DeviceIdType.MESH
F32 = jnp.float32
BF16 = jnp.bfloat16
CHUNKS = 4


def in_hbm(array):
    return pltpu.with_memory_space_constraint(array, pltpu.HBM)


def split(value):
    high = value.astype(BF16)
    return high, (value - high.astype(F32)).astype(BF16)


def kernel(
    n_cls, n_y, n_z,
    x_hbm, leaf_hbm, label_hbm,
    lv_out, x_v, onehot,
    leaf_v, label_v, e_v, stats, onehot_t, terms, sums, near, far, lv_t,
    load_sem, s_send, s_recv, r_send, r_recv, f_send, f_recv, g_send, g_recv,
):
    row, cls = lax.axis_index("rows"), lax.axis_index("cls")
    z, y = row // n_y, row % n_y
    half, odd = z // 2, z % 2
    n_half = n_z // 2
    rows, width = x_v.shape
    blocks = rows // LANES
    per_chunk = blocks // CHUNKS
    chunk_rows = rows // CHUNKS

    def cls_peer(d):
        return {"rows": row, "cls": lax.rem(cls + d, n_cls)}

    def near_place(j):
        dy, flip = j // 2, j % 2
        return lax.rem(y + dy, n_y), (1 - odd if flip else odd)

    def near_peer(j):
        to_y, to_odd = near_place(j)
        return {"rows": (half * 2 + to_odd) * n_y + to_y, "cls": cls}

    def far_peer(d):
        return {"rows": (lax.rem(half + d, n_half) * 2 + odd) * n_y + y, "cls": cls}

    loads = []
    for c in range(CHUNKS):
        part = pl.ds(c * chunk_rows, chunk_rows)
        loads.append(pltpu.make_async_copy(x_hbm.at[part], x_v.at[part], load_sem.at[c]))
    loads.append(pltpu.make_async_copy(leaf_hbm, leaf_v, load_sem.at[CHUNKS]))
    loads.append(pltpu.make_async_copy(label_hbm, label_v, load_sem.at[CHUNKS + 1]))
    for load in loads:
        load.start()

    barrier = pltpu.get_barrier_semaphore()
    for d in range(1, n_cls):
        pl.semaphore_signal(barrier, inc=1, device_id=cls_peer(d), device_id_type=MESH)
    for j in range(1, 2 * n_y):
        pl.semaphore_signal(barrier, inc=1, device_id=near_peer(j), device_id_type=MESH)
    for d in range(1, n_half):
        pl.semaphore_signal(barrier, inc=1, device_id=far_peer(d), device_id_type=MESH)

    exchanges = []
    for c in range(CHUNKS):
        loads[c].wait()

        def local(i, carry, c=c):
            at = pl.ds(pl.multiple_of((c * per_chunk + i) * LANES, LANES), LANES)
            xt = x_v[at, :].T
            peak = jnp.max(xt, axis=0, keepdims=True)
            expo = jnp.exp(xt - peak)
            e_v[:, at] = expo
            stats[0, c, 0, pl.ds(i, 1), :] = peak
            stats[0, c, 1, pl.ds(i, 1), :] = jnp.sum(expo, axis=0, keepdims=True)
            return carry

        lax.fori_loop(0, per_chunk, local, 0, unroll=4)
        if c == 0:
            pl.semaphore_wait(barrier, n_cls + 2 * n_y + n_half - 3)
        for d in range(1, n_cls):
            copy = pltpu.make_async_remote_copy(
                stats.at[0, c], stats.at[d, c], s_send.at[d, c], s_recv.at[d, c],
                device_id=cls_peer(d), device_id_type=MESH,
            )
            copy.start()
            exchanges.append(copy)

    loads[CHUNKS].wait()
    loads[CHUNKS + 1].wait()

    def one_hot_t(i, carry):
        at = pl.ds(pl.multiple_of(i * LANES, LANES), LANES)
        which = lax.broadcasted_iota(jnp.int32, (LEAVES, LANES), 0)
        onehot_t[:, at] = (which == leaf_v[pl.ds(i, 1), :]).astype(F32).astype(BF16)
        return carry

    lax.fori_loop(0, blocks, one_hot_t, 0, unroll=4)

    for c in range(CHUNKS):
        for d in range(1, n_cls):
            exchanges[c * (n_cls - 1) + d - 1].wait()
        peak = stats[0, c, 0]
        for d in range(1, n_cls):
            peak = jnp.maximum(peak, stats[d, c, 0])
        own = jnp.exp(stats[0, c, 0] - peak)
        total = stats[0, c, 1] * own
        for d in range(1, n_cls):
            total = total + stats[d, c, 1] * jnp.exp(stats[d, c, 0] - peak)
        stats[0, c, 1] = own / total

        def derive(i, carry, c=c):
            k = c * per_chunk + i
            at = pl.ds(pl.multiple_of(k * LANES, LANES), LANES)
            prob = e_v[:, at] * stats[0, c, 1, pl.ds(i, 1), :]
            classes = lax.broadcasted_iota(jnp.int32, (width, LANES), 0) + cls * width
            grad = prob - (classes == label_v[pl.ds(k, 1), :]).astype(F32)
            hess = prob * (1.0 - prob)
            terms[0:width, at], terms[width : 2 * width, at] = split(grad)
            terms[2 * width : 3 * width, at], terms[3 * width : 4 * width, at] = split(hess)
            return carry

        lax.fori_loop(0, per_chunk, derive, 0, unroll=4)

    acc = lax.dot_general(
        terms[...], onehot_t[...], (((1,), (1,)), ((), ())), preferred_element_type=F32
    )
    sums[0] = acc[0:width] + acc[width : 2 * width]
    sums[1] = acc[2 * width : 3 * width] + acc[3 * width : 4 * width]

    piece = width // (2 * n_y)
    copies = []
    for j in range(1, 2 * n_y):
        to_y, to_odd = near_place(j)
        theirs = pl.ds(pl.multiple_of((to_y * 2 + to_odd) * piece, piece), piece)
        copy = pltpu.make_async_remote_copy(
            sums.at[:, theirs], near.at[j], r_send.at[j], r_recv.at[j],
            device_id=near_peer(j), device_id_type=MESH,
        )
        copy.start()
        copies.append(copy)
    mine = y * 2 + odd
    total = sums[:, pl.ds(pl.multiple_of(mine * piece, piece), piece), :]
    for j in range(1, 2 * n_y):
        copies[j - 1].wait()
        total = total + near[j]
    far[half] = total

    copies = []
    for d in sorted(range(1, n_half), key=lambda d: abs(n_half - 2 * d)):
        copy = pltpu.make_async_remote_copy(
            far.at[half], far.at[half], f_send.at[d], f_recv.at[d],
            device_id=far_peer(d), device_id_type=MESH,
        )
        copy.start()
        copies.append(copy)

    def one_hot(i, carry):
        at = pl.ds(pl.multiple_of(i * LANES, LANES), LANES)
        hot = onehot_t[:, at].T
        onehot[at, 0:LEAVES] = hot
        onehot[at, LEAVES : 2 * LEAVES] = hot
        return carry

    lax.fori_loop(0, blocks, one_hot, 0, unroll=2)

    for d in range(1, n_half):
        source = lax.rem(half + n_half - d, n_half)
        pltpu.make_async_remote_copy(
            far.at[source], far.at[source], f_send.at[d], f_recv.at[d],
            device_id=far_peer(d), device_id_type=MESH,
        ).wait_recv()
    total = far[0]
    for k in range(1, n_half):
        total = total + far[k]
    lv_t[mine] = -0.3 * total[0] / (total[1] + 1.0)

    for j in range(1, 2 * n_y):
        copy = pltpu.make_async_remote_copy(
            lv_t.at[mine], lv_t.at[mine], g_send.at[j], g_recv.at[j],
            device_id=near_peer(j), device_id_type=MESH,
        )
        copy.start()
        copies.append(copy)
    for j in range(1, 2 * n_y):
        dy, flip = j // 2, j % 2
        source = lax.rem(y + n_y - dy, n_y) * 2 + (1 - odd if flip else odd)
        pltpu.make_async_remote_copy(
            lv_t.at[source], lv_t.at[source], g_send.at[j], g_recv.at[j],
            device_id=near_peer(j), device_id_type=MESH,
        ).wait_recv()
    lv_out[...] = lv_t[...].reshape(width, LEAVES).T
    for copy in copies:
        copy.wait_send()


def update(x_v, onehot, lv, lv_hbm, up_hbm, up_v, sem):
    values = jnp.concatenate(split(lv[...]), axis=0)
    copies = [pltpu.make_async_copy(lv, lv_hbm, sem.at[CHUNKS])]
    copies[0].start()
    chunk_rows = x_v.shape[0] // CHUNKS
    for c in range(CHUNKS):
        def part(i, carry, c=c):
            at = pl.ds(pl.multiple_of(c * chunk_rows + i * 256, 256), 256)
            up_v[at, :] = x_v[at, :] + jnp.dot(onehot[at, :], values, preferred_element_type=F32)
            return carry

        lax.fori_loop(0, chunk_rows // 256, part, 0, unroll=2)
        at = pl.ds(c * chunk_rows, chunk_rows)
        copies.append(pltpu.make_async_copy(up_v.at[at], up_hbm.at[at], sem.at[c]))
        copies[-1].start()
    for copy in copies:
        copy.wait()


def solution(mesh):
    n_cls, n_rows = mesh.shape["cls"], mesh.shape["rows"]
    n_y = 4
    n_z = n_rows // n_y

    def per_device(logits, leaf_index, labels):
        rows, width = logits.shape
        blocks = rows // LANES
        piece = width // (2 * n_y)
        dma = pltpu.SemaphoreType.DMA
        vmem = pl.BlockSpec(memory_space=pltpu.VMEM)
        hbm = pl.BlockSpec(memory_space=pltpu.HBM)
        leaf_values, x_v, onehot = pl.pallas_call(
            functools.partial(kernel, n_cls, n_y, n_z),
            out_shape=(
                pltpu.VMEM((LEAVES, width), F32),
                pltpu.VMEM((rows, width), F32),
                pltpu.VMEM((rows, 2 * LEAVES), BF16),
            ),
            in_specs=[hbm, hbm, hbm],
            out_specs=(vmem, vmem, vmem),
            scratch_shapes=[
                pltpu.VMEM((blocks, LANES), jnp.int32),
                pltpu.VMEM((blocks, LANES), jnp.int32),
                pltpu.VMEM((width, rows), F32),
                pltpu.VMEM((n_cls, CHUNKS, 2, blocks // CHUNKS, LANES), F32),
                pltpu.VMEM((LEAVES, rows), BF16),
                pltpu.VMEM((4 * width, rows), BF16),
                pltpu.VMEM((2, width, LEAVES), F32),
                pltpu.VMEM((2 * n_y, 2, piece, LEAVES), F32),
                pltpu.VMEM((n_z // 2, 2, piece, LEAVES), F32),
                pltpu.VMEM((2 * n_y, piece, LEAVES), F32),
                dma((CHUNKS + 2,)),
                dma((n_cls, CHUNKS)),
                dma((n_cls, CHUNKS)),
                dma((2 * n_y,)),
                dma((2 * n_y,)),
                dma((n_z // 2,)),
                dma((n_z // 2,)),
                dma((2 * n_y,)),
                dma((2 * n_y,)),
            ],
            compiler_params=pltpu.CompilerParams(
                collective_id=0, has_side_effects=True, vmem_limit_bytes=32 * 2**20
            ),
        )(
            in_hbm(logits),
            in_hbm(leaf_index.reshape(blocks, LANES)),
            in_hbm(labels.reshape(blocks, LANES)),
        )
        return pl.pallas_call(
            update,
            out_shape=(
                pltpu.HBM((LEAVES, width), F32),
                pltpu.HBM((rows, width), F32),
            ),
            in_specs=[vmem, vmem, vmem],
            out_specs=(hbm, hbm),
            scratch_shapes=[pltpu.VMEM((rows, width), F32), dma((CHUNKS + 1,))],
            compiler_params=pltpu.CompilerParams(vmem_limit_bytes=16 * 2**20),
        )(x_v, onehot, leaf_values)

    return jax.shard_map(
        per_device,
        mesh=mesh,
        in_specs=(P("rows", "cls"), P("rows"), P("rows")),
        out_specs=(P(None, "cls"), P("rows", "cls")),
        check_vma=False,
    )
```

time: 57.9 us -> 44.2 us (0.76)
  the two profiles are of different devices: /device:TPU:6 before, /device:TPU:1 now
where the time goes in v2:
time: 44.2 us; the launch traced here: 44 us
  Pallas kernels  43.4 us (98%)
  between operations  0.64 us (1%)
    pallas_call x1, Pallas kernels, per_device(): pl.pallas_call(functools.partial(kernel, n_cls, n_y, n_z), out_shape=(plt...  40.8 us
    pallas_call x1, Pallas kernels, per_device(): pl.pallas_call(update, out_shape=(pltpu.HBM((LEAVES, width), F32), pltpu....  2.55 us

profile of v2, /device:TPU:1, one launch (start us, length us, event | category | flops | bytes accessed | tf_op | source)
XLA Modules:
  0.0 44.0 jit_solution(3852566816771152782)
XLA Ops:
  0.6 40.8 %shard_map.50 = (f32[128,128]{1,0:T(8,128)S(1)}, f32[4096,128]{1,0:T(8,128)S(1)}, bf16[4096,256]{1,0:T(8,128)(2,1)S(1)}) custom-call(f32[4096,128]{1,0:T(8,128)} %x_hbm.1, s32[32,128]{1,0:T(8,128)} %bitcast.2, s32[32,128]{1,0:T(8,128)} %bitcast.3), custom_call_target="tpu_custom_call" | custom-call | tf_op jit(solution)/shard_map/pallas_call | solution.py:238
  41.5 2.5 %shard_map.51 = (f32[128,128]{1,0:T(8,128)}, f32[4096,128]{1,0:T(8,128)}) custom-call(f32[4096,128]{1,0:T(8,128)S(1)} %get-tuple-element.5.x_v, bf16[4096,256]{1,0:T(8,128)(2,1)S(1)} %get-tuple-element.6.onehot, f32[128,128]{1,0:T(8,128)S(1)} %get-tuple-element.7.lv), custom_call_target="tpu_custom_call" | custom-call | tf_op jit(solution)/shard_map/pallas_call | solution.py:276

commit v3 on v2

--- a/solution.py
+++ b/solution.py
@@ -13,6 +13,8 @@
 F32 = jnp.float32
 BF16 = jnp.bfloat16
 CHUNKS = 4
+PARTS = 2
+WRITES = 8
 
 
 def in_hbm(array):
@@ -28,8 +30,8 @@
     n_cls, n_y, n_z,
     x_hbm, leaf_hbm, label_hbm,
     lv_out, x_v, onehot,
-    leaf_v, label_v, e_v, stats, onehot_t, terms, sums, near, far, lv_t,
-    load_sem, s_send, s_recv, r_send, r_recv, f_send, f_recv, g_send, g_recv,
+    leaf_v, label_v, e_v, stats, chip, onehot_t, terms, sums, near, far, lv_t,
+    load_sem, c_send, c_recv, s_send, s_recv, r_send, r_recv, f_send, f_recv, g_send, g_recv,
 ):
     row, cls = lax.axis_index("rows"), lax.axis_index("cls")
     z, y = row // n_y, row % n_y
@@ -40,8 +42,14 @@
     per_chunk = blocks // CHUNKS
     chunk_rows = rows // CHUNKS
 
-    def cls_peer(d):
-        return {"rows": row, "cls": lax.rem(cls + d, n_cls)}
+    core = cls % 2
+    n_x = n_cls // 2
+
+    def core_peer():
+        return {"rows": row, "cls": cls + 1 - 2 * core}
+
+    def x_peer(d):
+        return {"rows": row, "cls": lax.rem(cls + 2 * d, n_cls)}
 
     def near_place(j):
         dy, flip = j // 2, j % 2
@@ -64,37 +72,32 @@
         load.start()
 
     barrier = pltpu.get_barrier_semaphore()
-    for d in range(1, n_cls):
-        pl.semaphore_signal(barrier, inc=1, device_id=cls_peer(d), device_id_type=MESH)
+    for d in range(1, n_x):
+        pl.semaphore_signal(barrier, inc=1, device_id=x_peer(d), device_id_type=MESH)
+    pl.semaphore_signal(barrier, inc=1, device_id=core_peer(), device_id_type=MESH)
+    for d in range(1, n_half):
+        pl.semaphore_signal(barrier, inc=1, device_id=far_peer(d), device_id_type=MESH)
     for j in range(1, 2 * n_y):
         pl.semaphore_signal(barrier, inc=1, device_id=near_peer(j), device_id_type=MESH)
-    for d in range(1, n_half):
-        pl.semaphore_signal(barrier, inc=1, device_id=far_peer(d), device_id_type=MESH)
-
-    exchanges = []
+
+    per_part = blocks // PARTS
     for c in range(CHUNKS):
         loads[c].wait()
 
         def local(i, carry, c=c):
-            at = pl.ds(pl.multiple_of((c * per_chunk + i) * LANES, LANES), LANES)
+            k = c * per_chunk + i
+            at = pl.ds(pl.multiple_of(k * LANES, LANES), LANES)
             xt = x_v[at, :].T
             peak = jnp.max(xt, axis=0, keepdims=True)
             expo = jnp.exp(xt - peak)
             e_v[:, at] = expo
-            stats[0, c, 0, pl.ds(i, 1), :] = peak
-            stats[0, c, 1, pl.ds(i, 1), :] = jnp.sum(expo, axis=0, keepdims=True)
+            h = c * per_chunk // per_part
+            at = pl.ds(k - h * per_part, 1)
+            stats[0, h, 0, at, :] = peak
+            stats[0, h, 1, at, :] = jnp.sum(expo, axis=0, keepdims=True)
             return carry
 
-        lax.fori_loop(0, per_chunk, local, 0, unroll=4)
-        if c == 0:
-            pl.semaphore_wait(barrier, n_cls + 2 * n_y + n_half - 3)
-        for d in range(1, n_cls):
-            copy = pltpu.make_async_remote_copy(
-                stats.at[0, c], stats.at[d, c], s_send.at[d, c], s_recv.at[d, c],
-                device_id=cls_peer(d), device_id_type=MESH,
-            )
-            copy.start()
-            exchanges.append(copy)
+        lax.fori_loop(0, per_chunk, local, 0, unroll=8)
 
     loads[CHUNKS].wait()
     loads[CHUNKS + 1].wait()
@@ -107,22 +110,64 @@
 
     lax.fori_loop(0, blocks, one_hot_t, 0, unroll=4)
 
-    for c in range(CHUNKS):
-        for d in range(1, n_cls):
-            exchanges[c * (n_cls - 1) + d - 1].wait()
-        peak = stats[0, c, 0]
-        for d in range(1, n_cls):
-            peak = jnp.maximum(peak, stats[d, c, 0])
-        own = jnp.exp(stats[0, c, 0] - peak)
-        total = stats[0, c, 1] * own
-        for d in range(1, n_cls):
-            total = total + stats[d, c, 1] * jnp.exp(stats[d, c, 0] - peak)
-        stats[0, c, 1] = own / total
-
-        def derive(i, carry, c=c):
-            k = c * per_chunk + i
+    pl.semaphore_wait(barrier, n_x + 2 * n_y + n_half - 2)
+    swaps = []
+    for h in range(PARTS):
+        copy = pltpu.make_async_remote_copy(
+            stats.at[0, h], stats.at[1, h], c_send.at[h], c_recv.at[h],
+            device_id=core_peer(), device_id_type=MESH,
+        )
+        copy.start()
+        swaps.append(copy)
+    exchanges = []
+    for h in range(PARTS):
+        swaps[h].wait()
+        peak = jnp.maximum(stats[0, h, 0], stats[1, h, 0])
+        chip[0, h, 0] = peak
+        chip[0, h, 1] = (
+            stats[0, h, 1] * jnp.exp(stats[0, h, 0] - peak)
+            + stats[1, h, 1] * jnp.exp(stats[1, h, 0] - peak)
+        )
+        for d in range(1, n_x):
+            copy = pltpu.make_async_remote_copy(
+                chip.at[0, h], chip.at[d, h], s_send.at[d, h], s_recv.at[d, h],
+                device_id=x_peer(d), device_id_type=MESH,
+            )
+            copy.start()
+            exchanges.append(copy)
+
+    piece = width // (2 * n_y)
+
+    def share(g):
+        copies = []
+        for j in near_order:
+            to_y, to_odd = near_place(j)
+            theirs = pl.ds(pl.multiple_of((to_y * 2 + to_odd) * piece, piece), piece)
+            copy = pltpu.make_async_remote_copy(
+                sums.at[g, theirs], near.at[j, g], r_send.at[j, g], r_recv.at[j, g],
+                device_id=near_peer(j), device_id_type=MESH,
+            )
+            copy.start()
+            copies.append(copy)
+        return copies
+
+    near_order = sorted(range(1, 2 * n_y), key=lambda j: -(min(j // 2, n_y - j // 2) + j % 2))
+    shares = []
+    for h in range(PARTS):
+        for d in range(1, n_x):
+            exchanges[h * (n_x - 1) + d - 1].wait()
+        peak = chip[0, h, 0]
+        for d in range(1, n_x):
+            peak = jnp.maximum(peak, chip[d, h, 0])
+        total = chip[0, h, 1] * jnp.exp(chip[0, h, 0] - peak)
+        for d in range(1, n_x):
+            total = total + chip[d, h, 1] * jnp.exp(chip[d, h, 0] - peak)
+        stats[0, h, 1] = jnp.exp(stats[0, h, 0] - peak) / total
+
+        def derive(i, carry, h=h):
+            k = h * per_part + i
             at = pl.ds(pl.multiple_of(k * LANES, LANES), LANES)
-            prob = e_v[:, at] * stats[0, c, 1, pl.ds(i, 1), :]
+            prob = e_v[:, at] * stats[0, h, 1, pl.ds(i, 1), :]
             classes = lax.broadcasted_iota(jnp.int32, (width, LANES), 0) + cls * width
             grad = prob - (classes == label_v[pl.ds(k, 1), :]).astype(F32)
             hess = prob * (1.0 - prob)
@@ -130,37 +175,37 @@
             terms[2 * width : 3 * width, at], terms[3 * width : 4 * width, at] = split(hess)
             return carry
 
-        lax.fori_loop(0, per_chunk, derive, 0, unroll=4)
-
-    acc = lax.dot_general(
-        terms[...], onehot_t[...], (((1,), (1,)), ((), ())), preferred_element_type=F32
-    )
-    sums[0] = acc[0:width] + acc[width : 2 * width]
-    sums[1] = acc[2 * width : 3 * width] + acc[3 * width : 4 * width]
-
-    piece = width // (2 * n_y)
+        lax.fori_loop(0, per_part, derive, 0, unroll=4)
+
+        part = slice(h * per_part * LANES, (h + 1) * per_part * LANES)
+        for g in range(2):
+            acc = lax.dot_general(
+                terms[2 * g * width : 2 * (g + 1) * width, part],
+                onehot_t[:, part],
+                (((1,), (1,)), ((), ())),
+                preferred_element_type=F32,
+            )
+            acc = acc[0:width] + acc[width : 2 * width]
+            sums[g] = acc if h == 0 else sums[g] + acc
+            if h == PARTS - 1:
+                shares.append(share(g))
+
+    mine = y * 2 + odd
+    own_part = pl.ds(pl.multiple_of(mine * piece, piece), piece)
+    for g in range(2):
+        for copy in shares[g]:
+            copy.wait()
+        total = sums[g, own_part, :]
+        for j in range(1, 2 * n_y):
+            total = total + near[j, g]
+        far[half, g] = total
+
     copies = []
-    for j in range(1, 2 * n_y):
-        to_y, to_odd = near_place(j)
-        theirs = pl.ds(pl.multiple_of((to_y * 2 + to_odd) * piece, piece), piece)
+    for k in range(n_half - 1):
+        to = jnp.where(half <= k, k + 1, k)
         copy = pltpu.make_async_remote_copy(
-            sums.at[:, theirs], near.at[j], r_send.at[j], r_recv.at[j],
-            device_id=near_peer(j), device_id_type=MESH,
-        )
-        copy.start()
-        copies.append(copy)
-    mine = y * 2 + odd
-    total = sums[:, pl.ds(pl.multiple_of(mine * piece, piece), piece), :]
-    for j in range(1, 2 * n_y):
-        copies[j - 1].wait()
-        total = total + near[j]
-    far[half] = total
-
-    copies = []
-    for d in sorted(range(1, n_half), key=lambda d: abs(n_half - 2 * d)):
-        copy = pltpu.make_async_remote_copy(
-            far.at[half], far.at[half], f_send.at[d], f_recv.at[d],
-            device_id=far_peer(d), device_id_type=MESH,
+            far.at[half], far.at[half], f_send.at[k], f_recv.at[half],
+            device_id={"rows": (to * 2 + odd) * n_y + y, "cls": cls}, device_id_type=MESH,
         )
         copy.start()
         copies.append(copy)
@@ -172,12 +217,12 @@
         onehot[at, LEAVES : 2 * LEAVES] = hot
         return carry
 
-    lax.fori_loop(0, blocks, one_hot, 0, unroll=2)
+    lax.fori_loop(0, blocks, one_hot, 0, unroll=8)
 
     for d in range(1, n_half):
         source = lax.rem(half + n_half - d, n_half)
         pltpu.make_async_remote_copy(
-            far.at[source], far.at[source], f_send.at[d], f_recv.at[d],
+            far.at[source], far.at[source], f_send.at[d], f_recv.at[source],
             device_id=far_peer(d), device_id_type=MESH,
         ).wait_recv()
     total = far[0]
@@ -185,7 +230,7 @@
         total = total + far[k]
     lv_t[mine] = -0.3 * total[0] / (total[1] + 1.0)
 
-    for j in range(1, 2 * n_y):
+    for j in near_order:
         copy = pltpu.make_async_remote_copy(
             lv_t.at[mine], lv_t.at[mine], g_send.at[j], g_recv.at[j],
             device_id=near_peer(j), device_id_type=MESH,
@@ -206,10 +251,10 @@
 
 def update(x_v, onehot, lv, lv_hbm, up_hbm, up_v, sem):
     values = jnp.concatenate(split(lv[...]), axis=0)
-    copies = [pltpu.make_async_copy(lv, lv_hbm, sem.at[CHUNKS])]
+    copies = [pltpu.make_async_copy(lv, lv_hbm, sem.at[WRITES])]
     copies[0].start()
-    chunk_rows = x_v.shape[0] // CHUNKS
-    for c in range(CHUNKS):
+    chunk_rows = x_v.shape[0] // WRITES
+    for c in range(WRITES):
         def part(i, carry, c=c):
             at = pl.ds(pl.multiple_of(c * chunk_rows + i * 256, 256), 256)
             up_v[at, :] = x_v[at, :] + jnp.dot(onehot[at, :], values, preferred_element_type=F32)
@@ -248,7 +293,8 @@
                 pltpu.VMEM((blocks, LANES), jnp.int32),
                 pltpu.VMEM((blocks, LANES), jnp.int32),
                 pltpu.VMEM((width, rows), F32),
-                pltpu.VMEM((n_cls, CHUNKS, 2, blocks // CHUNKS, LANES), F32),
+                pltpu.VMEM((2, PARTS, 2, blocks // PARTS, LANES), F32),
+                pltpu.VMEM((n_cls // 2, PARTS, 2, blocks // PARTS, LANES), F32),
                 pltpu.VMEM((LEAVES, rows), BF16),
                 pltpu.VMEM((4 * width, rows), BF16),
                 pltpu.VMEM((2, width, LEAVES), F32),
@@ -256,10 +302,12 @@
                 pltpu.VMEM((n_z // 2, 2, piece, LEAVES), F32),
                 pltpu.VMEM((2 * n_y, piece, LEAVES), F32),
                 dma((CHUNKS + 2,)),
-                dma((n_cls, CHUNKS)),
-                dma((n_cls, CHUNKS)),
-                dma((2 * n_y,)),
-                dma((2 * n_y,)),
+                dma((PARTS,)),
+                dma((PARTS,)),
+                dma((n_cls // 2, PARTS)),
+                dma((n_cls // 2, PARTS)),
+                dma((2 * n_y, 2)),
+                dma((2 * n_y, 2)),
                 dma((n_z // 2,)),
                 dma((n_z // 2,)),
                 dma((2 * n_y,)),
@@ -281,7 +329,7 @@
             ),
             in_specs=[vmem, vmem, vmem],
             out_specs=(hbm, hbm),
-            scratch_shapes=[pltpu.VMEM((rows, width), F32), dma((CHUNKS + 1,))],
+            scratch_shapes=[pltpu.VMEM((rows, width), F32), dma((WRITES + 1,))],
             compiler_params=pltpu.CompilerParams(vmem_limit_bytes=16 * 2**20),
         )(x_v, onehot, leaf_values)
 

time: 44.2 us -> 42.6 us (0.964)
  the two profiles are of different devices: /device:TPU:1 before, /device:TPU:32 now
where the time goes in v3:
time: 42.6 us; the launch traced here: 42.4 us
  Pallas kernels  41.8 us (98%)
  between operations  0.64 us (2%)
    pallas_call x1, Pallas kernels, per_device(): pl.pallas_call(functools.partial(kernel, n_cls, n_y, n_z), out_shape=(plt...  40.2 us
    pallas_call x1, Pallas kernels, per_device(): pl.pallas_call(update, out_shape=(pltpu.HBM((LEAVES, width), F32), pltpu....  1.6 us

profile of v3, /device:TPU:32, one launch (start us, length us, event | category | flops | bytes accessed | tf_op | source)
XLA Modules:
  0.0 42.4 jit_solution(6370345196069020924)
XLA Ops:
  0.6 40.2 %shard_map.50 = (f32[128,128]{1,0:T(8,128)S(1)}, f32[4096,128]{1,0:T(8,128)S(1)}, bf16[4096,256]{1,0:T(8,128)(2,1)S(1)}) custom-call(f32[4096,128]{1,0:T(8,128)} %x_hbm.1, s32[32,128]{1,0:T(8,128)} %bitcast.2, s32[32,128]{1,0:T(8,128)} %bitcast.3), custom_call_target="tpu_custom_call" | custom-call | tf_op jit(solution)/shard_map/pallas_call | solution.py:283
  40.8 1.6 %shard_map.51 = (f32[128,128]{1,0:T(8,128)}, f32[4096,128]{1,0:T(8,128)}) custom-call(f32[4096,128]{1,0:T(8,128)S(1)} %get-tuple-element.5.x_v, bf16[4096,256]{1,0:T(8,128)(2,1)S(1)} %get-tuple-element.6.onehot, f32[128,128]{1,0:T(8,128)S(1)} %get-tuple-element.7.lv), custom_call_target="tpu_custom_call" | custom-call | tf_op jit(solution)/shard_map/pallas_call | solution.py:324

commit v4 on v3

--- a/solution.py
+++ b/solution.py
@@ -14,6 +14,7 @@
 BF16 = jnp.bfloat16
 CHUNKS = 4
 PARTS = 2
+TOGETHER = 4
 WRITES = 8
 
 
@@ -30,7 +31,7 @@
     n_cls, n_y, n_z,
     x_hbm, leaf_hbm, label_hbm,
     lv_out, x_v, onehot,
-    leaf_v, label_v, e_v, stats, chip, onehot_t, terms, sums, near, far, lv_t,
+    leaf_v, label_v, e_v, stats, chip, onehot_t, sums, near, far, lv_t,
     load_sem, c_send, c_recv, s_send, s_recv, r_send, r_recv, f_send, f_recv, g_send, g_recv,
 ):
     row, cls = lax.axis_index("rows"), lax.axis_index("cls")
@@ -99,17 +100,6 @@
 
         lax.fori_loop(0, per_chunk, local, 0, unroll=8)
 
-    loads[CHUNKS].wait()
-    loads[CHUNKS + 1].wait()
-
-    def one_hot_t(i, carry):
-        at = pl.ds(pl.multiple_of(i * LANES, LANES), LANES)
-        which = lax.broadcasted_iota(jnp.int32, (LEAVES, LANES), 0)
-        onehot_t[:, at] = (which == leaf_v[pl.ds(i, 1), :]).astype(F32).astype(BF16)
-        return carry
-
-    lax.fori_loop(0, blocks, one_hot_t, 0, unroll=4)
-
     pl.semaphore_wait(barrier, n_x + 2 * n_y + n_half - 2)
     swaps = []
     for h in range(PARTS):
@@ -136,23 +126,22 @@
             copy.start()
             exchanges.append(copy)
 
+    loads[CHUNKS].wait()
+    loads[CHUNKS + 1].wait()
+
+    def one_hot_t(i, carry):
+        at = pl.ds(pl.multiple_of(i * LANES, LANES), LANES)
+        which = lax.broadcasted_iota(jnp.int32, (LEAVES, LANES), 0)
+        onehot_t[:, at] = (which == leaf_v[pl.ds(i, 1), :]).astype(F32).astype(BF16)
+        return carry
+
+    lax.fori_loop(0, blocks, one_hot_t, 0, unroll=4)
+
     piece = width // (2 * n_y)
 
-    def share(g):
-        copies = []
-        for j in near_order:
-            to_y, to_odd = near_place(j)
-            theirs = pl.ds(pl.multiple_of((to_y * 2 + to_odd) * piece, piece), piece)
-            copy = pltpu.make_async_remote_copy(
-                sums.at[g, theirs], near.at[j, g], r_send.at[j, g], r_recv.at[j, g],
-                device_id=near_peer(j), device_id_type=MESH,
-            )
-            copy.start()
-            copies.append(copy)
-        return copies
-
     near_order = sorted(range(1, 2 * n_y), key=lambda j: -(min(j // 2, n_y - j // 2) + j % 2))
-    shares = []
+    classes = lax.broadcasted_iota(jnp.int32, (width, LANES), 0) + cls * width
+    acc = None
     for h in range(PARTS):
         for d in range(1, n_x):
             exchanges[h * (n_x - 1) + d - 1].wait()
@@ -164,41 +153,43 @@
             total = total + chip[d, h, 1] * jnp.exp(chip[d, h, 0] - peak)
         stats[0, h, 1] = jnp.exp(stats[0, h, 0] - peak) / total
 
-        def derive(i, carry, h=h):
-            k = h * per_part + i
-            at = pl.ds(pl.multiple_of(k * LANES, LANES), LANES)
-            prob = e_v[:, at] * stats[0, h, 1, pl.ds(i, 1), :]
-            classes = lax.broadcasted_iota(jnp.int32, (width, LANES), 0) + cls * width
-            grad = prob - (classes == label_v[pl.ds(k, 1), :]).astype(F32)
-            hess = prob * (1.0 - prob)
-            terms[0:width, at], terms[width : 2 * width, at] = split(grad)
-            terms[2 * width : 3 * width, at], terms[3 * width : 4 * width, at] = split(hess)
-            return carry
-
-        lax.fori_loop(0, per_part, derive, 0, unroll=4)
-
-        part = slice(h * per_part * LANES, (h + 1) * per_part * LANES)
-        for g in range(2):
-            acc = lax.dot_general(
-                terms[2 * g * width : 2 * (g + 1) * width, part],
-                onehot_t[:, part],
-                (((1,), (1,)), ((), ())),
-                preferred_element_type=F32,
+        for k in range(h * per_part, (h + 1) * per_part, TOGETHER):
+            grads, hessians = [], []
+            for i in range(k, k + TOGETHER):
+                at = slice(i * LANES, (i + 1) * LANES)
+                inverse = i - h * per_part
+                prob = e_v[:, at] * stats[0, h, 1, inverse : inverse + 1, :]
+                grads.append(prob - (classes == label_v[i : i + 1, :]).astype(F32))
+                hessians.append(prob * (1.0 - prob))
+            at = slice(k * LANES, (k + TOGETHER) * LANES)
+            terms = split(jnp.concatenate(grads, axis=1)) + split(jnp.concatenate(hessians, axis=1))
+            part = lax.dot_general(
+                jnp.concatenate(terms, axis=0), onehot_t[:, at],
+                (((1,), (1,)), ((), ())), preferred_element_type=F32,
             )
-            acc = acc[0:width] + acc[width : 2 * width]
-            sums[g] = acc if h == 0 else sums[g] + acc
-            if h == PARTS - 1:
-                shares.append(share(g))
+            acc = part if acc is None else acc + part
+    sums[0] = acc[0:width] + acc[width : 2 * width]
+    sums[1] = acc[2 * width : 3 * width] + acc[3 * width : 4 * width]
+
+    shares = []
+    for j in near_order:
+        to_y, to_odd = near_place(j)
+        theirs = pl.ds(pl.multiple_of((to_y * 2 + to_odd) * piece, piece), piece)
+        copy = pltpu.make_async_remote_copy(
+            sums.at[:, theirs], near.at[j], r_send.at[j], r_recv.at[j],
+            device_id=near_peer(j), device_id_type=MESH,
+        )
+        copy.start()
+        shares.append(copy)
 
     mine = y * 2 + odd
     own_part = pl.ds(pl.multiple_of(mine * piece, piece), piece)
-    for g in range(2):
-        for copy in shares[g]:
-            copy.wait()
-        total = sums[g, own_part, :]
-        for j in range(1, 2 * n_y):
-            total = total + near[j, g]
-        far[half, g] = total
+    for copy in shares:
+        copy.wait()
+    total = sums[:, own_part, :]
+    for j in range(1, 2 * n_y):
+        total = total + near[j]
+    far[half] = total
 
     copies = []
     for k in range(n_half - 1):
@@ -296,7 +287,6 @@
                 pltpu.VMEM((2, PARTS, 2, blocks // PARTS, LANES), F32),
                 pltpu.VMEM((n_cls // 2, PARTS, 2, blocks // PARTS, LANES), F32),
                 pltpu.VMEM((LEAVES, rows), BF16),
-                pltpu.VMEM((4 * width, rows), BF16),
                 pltpu.VMEM((2, width, LEAVES), F32),
                 pltpu.VMEM((2 * n_y, 2, piece, LEAVES), F32),
                 pltpu.VMEM((n_z // 2, 2, piece, LEAVES), F32),
@@ -306,8 +296,8 @@
                 dma((PARTS,)),
                 dma((n_cls // 2, PARTS)),
                 dma((n_cls // 2, PARTS)),
-                dma((2 * n_y, 2)),
-                dma((2 * n_y, 2)),
+                dma((2 * n_y,)),
+                dma((2 * n_y,)),
                 dma((n_z // 2,)),
                 dma((n_z // 2,)),
                 dma((2 * n_y,)),

time: 42.6 us -> 41.4 us (0.972)
  Pallas kernels: 41.8 us -> 40.6 us
    pallas_call x1, Pallas kernels: 40.2 us -> 39 us  [per_device(): pl.pallas_call(functools.partial(kernel, n_cls, n_y, n_z), out_shape=(plt...]
where the time goes in v4:
time: 41.4 us; the launch traced here: 41.3 us
  Pallas kernels  40.6 us (98%)
  between operations  0.64 us (2%)
    pallas_call x1, Pallas kernels, per_device(): pl.pallas_call(functools.partial(kernel, n_cls, n_y, n_z), out_shape=(plt...  39 us
    pallas_call x1, Pallas kernels, per_device(): pl.pallas_call(update, out_shape=(pltpu.HBM((LEAVES, width), F32), pltpu....  1.61 us

profile of v4, /device:TPU:32, one launch (start us, length us, event | category | flops | bytes accessed | tf_op | source)
XLA Modules:
  0.0 41.3 jit_solution(12105330125381536667)
XLA Ops:
  0.6 39.0 %shard_map.50 = (f32[128,128]{1,0:T(8,128)S(1)}, f32[4096,128]{1,0:T(8,128)S(1)}, bf16[4096,256]{1,0:T(8,128)(2,1)S(1)}) custom-call(f32[4096,128]{1,0:T(8,128)} %x_hbm.1, s32[32,128]{1,0:T(8,128)} %bitcast.2, s32[32,128]{1,0:T(8,128)} %bitcast.3), custom_call_target="tpu_custom_call" | custom-call | tf_op jit(solution)/shard_map/pallas_call | solution.py:274
  39.7 1.6 %shard_map.51 = (f32[128,128]{1,0:T(8,128)}, f32[4096,128]{1,0:T(8,128)}) custom-call(f32[4096,128]{1,0:T(8,128)S(1)} %get-tuple-element.5.x_v, bf16[4096,256]{1,0:T(8,128)(2,1)S(1)} %get-tuple-element.6.onehot, f32[128,128]{1,0:T(8,128)S(1)} %get-tuple-element.7.lv), custom_call_target="tpu_custom_call" | custom-call | tf_op jit(solution)/shard_map/pallas_call | solution.py:314

commit v5 on v4

--- a/solution.py
+++ b/solution.py
@@ -32,7 +32,7 @@
     x_hbm, leaf_hbm, label_hbm,
     lv_out, x_v, onehot,
     leaf_v, label_v, e_v, stats, chip, onehot_t, sums, near, far, lv_t,
-    load_sem, c_send, c_recv, s_send, s_recv, r_send, r_recv, f_send, f_recv, g_send, g_recv,
+    known, load_sem, c_send, c_recv, s_send, s_recv, r_send, r_recv, f_send, f_recv, g_send, g_recv,
 ):
     row, cls = lax.axis_index("rows"), lax.axis_index("cls")
     z, y = row // n_y, row % n_y
@@ -60,6 +60,9 @@
         to_y, to_odd = near_place(j)
         return {"rows": (half * 2 + to_odd) * n_y + to_y, "cls": cls}
 
+    def z_peer(d):
+        return {"rows": lax.rem(z + d + n_z, n_z) * n_y + y, "cls": cls}
+
     def far_peer(d):
         return {"rows": (lax.rem(half + d, n_half) * 2 + odd) * n_y + y, "cls": cls}
 
@@ -73,13 +76,24 @@
         load.start()
 
     barrier = pltpu.get_barrier_semaphore()
+    near_order = sorted(range(1, 2 * n_y), key=lambda j: -(min(j // 2, n_y - j // 2) + j % 2))
+    for j in near_order:
+        pl.semaphore_signal(barrier, inc=1, device_id=near_peer(j), device_id_type=MESH)
     for d in range(1, n_x):
         pl.semaphore_signal(barrier, inc=1, device_id=x_peer(d), device_id_type=MESH)
     pl.semaphore_signal(barrier, inc=1, device_id=core_peer(), device_id_type=MESH)
-    for d in range(1, n_half):
-        pl.semaphore_signal(barrier, inc=1, device_id=far_peer(d), device_id_type=MESH)
-    for j in range(1, 2 * n_y):
-        pl.semaphore_signal(barrier, inc=1, device_id=near_peer(j), device_id_type=MESH)
+    pl.semaphore_signal(barrier, inc=1, device_id=z_peer(2 * odd - 1), device_id_type=MESH)
+
+    def tell(step):
+        for side in range(2):
+            pl.semaphore_signal(
+                known.at[step, side], inc=1,
+                device_id=z_peer((1 - 2 * side) * 2**step), device_id_type=MESH,
+            )
+
+    def hear(step):
+        for side in range(2):
+            pl.semaphore_wait(known.at[step, side], 1)
 
     per_part = blocks // PARTS
     for c in range(CHUNKS):
@@ -100,7 +114,7 @@
 
         lax.fori_loop(0, per_chunk, local, 0, unroll=8)
 
-    pl.semaphore_wait(barrier, n_x + 2 * n_y + n_half - 2)
+    pl.semaphore_wait(barrier, n_x + 2 * n_y)
     swaps = []
     for h in range(PARTS):
         copy = pltpu.make_async_remote_copy(
@@ -109,6 +123,7 @@
         )
         copy.start()
         swaps.append(copy)
+    tell(0)
     exchanges = []
     for h in range(PARTS):
         swaps[h].wait()
@@ -137,9 +152,10 @@
 
     lax.fori_loop(0, blocks, one_hot_t, 0, unroll=4)
 
+    hear(0)
+    tell(1)
     piece = width // (2 * n_y)
 
-    near_order = sorted(range(1, 2 * n_y), key=lambda j: -(min(j // 2, n_y - j // 2) + j % 2))
     classes = lax.broadcasted_iota(jnp.int32, (width, LANES), 0) + cls * width
     acc = None
     for h in range(PARTS):
@@ -181,6 +197,8 @@
         )
         copy.start()
         shares.append(copy)
+    hear(1)
+    tell(2)
 
     mine = y * 2 + odd
     own_part = pl.ds(pl.multiple_of(mine * piece, piece), piece)
@@ -191,6 +209,7 @@
         total = total + near[j]
     far[half] = total
 
+    hear(2)
     copies = []
     for k in range(n_half - 1):
         to = jnp.where(half <= k, k + 1, k)
@@ -263,6 +282,7 @@
     n_cls, n_rows = mesh.shape["cls"], mesh.shape["rows"]
     n_y = 4
     n_z = n_rows // n_y
+    assert n_z == 16
 
     def per_device(logits, leaf_index, labels):
         rows, width = logits.shape
@@ -291,6 +311,7 @@
                 pltpu.VMEM((2 * n_y, 2, piece, LEAVES), F32),
                 pltpu.VMEM((n_z // 2, 2, piece, LEAVES), F32),
                 pltpu.VMEM((2 * n_y, piece, LEAVES), F32),
+                pltpu.SemaphoreType.REGULAR((3, 2)),
                 dma((CHUNKS + 2,)),
                 dma((PARTS,)),
                 dma((PARTS,)),

time: 41.4 us -> 39.5 us (0.954)
  the two profiles are of different devices: /device:TPU:32 before, /device:TPU:8 now
where the time goes in v5:
time: 39.5 us; the launch traced here: 39.4 us
  Pallas kernels  38.7 us (98%)
  between operations  0.64 us (2%)
    pallas_call x1, Pallas kernels, per_device(): pl.pallas_call(functools.partial(kernel, n_cls, n_y, n_z), out_shape=(plt...  37.1 us
    pallas_call x1, Pallas kernels, per_device(): pl.pallas_call(update, out_shape=(pltpu.HBM((LEAVES, width), F32), pltpu....  1.61 us

profile of v5, /device:TPU:8, one launch (start us, length us, event | category | flops | bytes accessed | tf_op | source)
XLA Modules:
  0.0 39.4 jit_solution(13706263169555805759)
XLA Ops:
  0.6 37.1 %shard_map.50 = (f32[128,128]{1,0:T(8,128)S(1)}, f32[4096,128]{1,0:T(8,128)S(1)}, bf16[4096,256]{1,0:T(8,128)(2,1)S(1)}) custom-call(f32[4096,128]{1,0:T(8,128)} %x_hbm.1, s32[32,128]{1,0:T(8,128)} %bitcast.2, s32[32,128]{1,0:T(8,128)} %bitcast.3), custom_call_target="tpu_custom_call" | custom-call | tf_op jit(solution)/shard_map/pallas_call | solution.py:294
  37.8 1.6 %shard_map.51 = (f32[128,128]{1,0:T(8,128)}, f32[4096,128]{1,0:T(8,128)}) custom-call(f32[4096,128]{1,0:T(8,128)S(1)} %get-tuple-element.5.x_v, bf16[4096,256]{1,0:T(8,128)(2,1)S(1)} %get-tuple-element.6.onehot, f32[128,128]{1,0:T(8,128)S(1)} %get-tuple-element.7.lv), custom_call_target="tpu_custom_call" | custom-call | tf_op jit(solution)/shard_map/pallas_call | solution.py:335

commit v6 on v5

--- a/solution.py
+++ b/solution.py
@@ -38,6 +38,11 @@
     z, y = row // n_y, row % n_y
     half, odd = z // 2, z % 2
     n_half = n_z // 2
+
+    def role_of(of_half, of_odd):
+        return lax.rem(of_odd + of_half // (n_half // 2), 2)
+
+    role = role_of(half, odd)
     rows, width = x_v.shape
     blocks = rows // LANES
     per_chunk = blocks // CHUNKS
@@ -54,17 +59,18 @@
 
     def near_place(j):
         dy, flip = j // 2, j % 2
-        return lax.rem(y + dy, n_y), (1 - odd if flip else odd)
+        return lax.rem(y + dy, n_y), (1 - role if flip else role)
 
     def near_peer(j):
-        to_y, to_odd = near_place(j)
-        return {"rows": (half * 2 + to_odd) * n_y + to_y, "cls": cls}
+        dy, flip = j // 2, j % 2
+        to_odd = 1 - odd if flip else odd
+        return {"rows": (half * 2 + to_odd) * n_y + lax.rem(y + dy, n_y), "cls": cls}
 
     def z_peer(d):
         return {"rows": lax.rem(z + d + n_z, n_z) * n_y + y, "cls": cls}
 
-    def far_peer(d):
-        return {"rows": (lax.rem(half + d, n_half) * 2 + odd) * n_y + y, "cls": cls}
+    def far_peer(to):
+        return {"rows": (to * 2 + role_of(to, role)) * n_y + y, "cls": cls}
 
     loads = []
     for c in range(CHUNKS):
@@ -189,8 +195,8 @@
 
     shares = []
     for j in near_order:
-        to_y, to_odd = near_place(j)
-        theirs = pl.ds(pl.multiple_of((to_y * 2 + to_odd) * piece, piece), piece)
+        to_y, to_role = near_place(j)
+        theirs = pl.ds(pl.multiple_of((to_y * 2 + to_role) * piece, piece), piece)
         copy = pltpu.make_async_remote_copy(
             sums.at[:, theirs], near.at[j], r_send.at[j], r_recv.at[j],
             device_id=near_peer(j), device_id_type=MESH,
@@ -200,7 +206,7 @@
     hear(1)
     tell(2)
 
-    mine = y * 2 + odd
+    mine = y * 2 + role
     own_part = pl.ds(pl.multiple_of(mine * piece, piece), piece)
     for copy in shares:
         copy.wait()
@@ -215,7 +221,7 @@
         to = jnp.where(half <= k, k + 1, k)
         copy = pltpu.make_async_remote_copy(
             far.at[half], far.at[half], f_send.at[k], f_recv.at[half],
-            device_id={"rows": (to * 2 + odd) * n_y + y, "cls": cls}, device_id_type=MESH,
+            device_id=far_peer(to), device_id_type=MESH,
         )
         copy.start()
         copies.append(copy)
@@ -233,7 +239,7 @@
         source = lax.rem(half + n_half - d, n_half)
         pltpu.make_async_remote_copy(
             far.at[source], far.at[source], f_send.at[d], f_recv.at[source],
-            device_id=far_peer(d), device_id_type=MESH,
+            device_id=far_peer(source), device_id_type=MESH,
         ).wait_recv()
     total = far[0]
     for k in range(1, n_half):
@@ -249,7 +255,7 @@
         copies.append(copy)
     for j in range(1, 2 * n_y):
         dy, flip = j // 2, j % 2
-        source = lax.rem(y + n_y - dy, n_y) * 2 + (1 - odd if flip else odd)
+        source = lax.rem(y + n_y - dy, n_y) * 2 + (1 - role if flip else role)
         pltpu.make_async_remote_copy(
             lv_t.at[source], lv_t.at[source], g_send.at[j], g_recv.at[j],
             device_id=near_peer(j), device_id_type=MESH,

time: 39.5 us -> 39.1 us (0.990)
  Pallas kernels: 38.7 us -> 38.3 us
    pallas_call x1, Pallas kernels: 37.1 us -> 36.7 us  [per_device(): pl.pallas_call(functools.partial(kernel, n_cls, n_y, n_z), out_shape=(plt...]
where the time goes in v6:
time: 39.1 us; the launch traced here: 38.9 us
  Pallas kernels  38.3 us (98%)
  between operations  0.64 us (2%)
    pallas_call x1, Pallas kernels, per_device(): pl.pallas_call(functools.partial(kernel, n_cls, n_y, n_z), out_shape=(plt...  36.7 us
    pallas_call x1, Pallas kernels, per_device(): pl.pallas_call(update, out_shape=(pltpu.HBM((LEAVES, width), F32), pltpu....  1.61 us

profile of v6, /device:TPU:8, one launch (start us, length us, event | category | flops | bytes accessed | tf_op | source)
XLA Modules:
  0.0 38.9 jit_solution(2067866998418053105)
XLA Ops:
  0.6 36.7 %shard_map.50 = (f32[128,128]{1,0:T(8,128)S(1)}, f32[4096,128]{1,0:T(8,128)S(1)}, bf16[4096,256]{1,0:T(8,128)(2,1)S(1)}) custom-call(f32[4096,128]{1,0:T(8,128)} %x_hbm.1, s32[32,128]{1,0:T(8,128)} %bitcast.2, s32[32,128]{1,0:T(8,128)} %bitcast.3), custom_call_target="tpu_custom_call" | custom-call | tf_op jit(solution)/shard_map/pallas_call | solution.py:300
  37.3 1.6 %shard_map.51 = (f32[128,128]{1,0:T(8,128)}, f32[4096,128]{1,0:T(8,128)}) custom-call(f32[4096,128]{1,0:T(8,128)S(1)} %get-tuple-element.5.x_v, bf16[4096,256]{1,0:T(8,128)(2,1)S(1)} %get-tuple-element.6.onehot, f32[128,128]{1,0:T(8,128)S(1)} %get-tuple-element.7.lv), custom_call_target="tpu_custom_call" | custom-call | tf_op jit(solution)/shard_map/pallas_call | solution.py:341

commit v7 on v6

--- a/solution.py
+++ b/solution.py
@@ -31,8 +31,8 @@
     n_cls, n_y, n_z,
     x_hbm, leaf_hbm, label_hbm,
     lv_out, x_v, onehot,
-    leaf_v, label_v, e_v, stats, chip, onehot_t, sums, near, far, lv_t,
-    known, load_sem, c_send, c_recv, s_send, s_recv, r_send, r_recv, f_send, f_recv, g_send, g_recv,
+    leaf_v, label_v, e_v, stats, chip, onehot_t, sums, near, far, other, lv_t,
+    known, load_sem, c_send, c_recv, s_send, s_recv, r_send, r_recv, f_send, f_recv, o_send, o_recv, g_send, g_recv,
 ):
     row, cls = lax.axis_index("rows"), lax.axis_index("cls")
     z, y = row // n_y, row % n_y
@@ -40,7 +40,7 @@
     n_half = n_z // 2
 
     def role_of(of_half, of_odd):
-        return lax.rem(of_odd + of_half // (n_half // 2), 2)
+        return jnp.where(of_half == n_half // 2, 1 - of_odd, of_odd)
 
     role = role_of(half, odd)
     rows, width = x_v.shape
@@ -225,6 +225,13 @@
         )
         copy.start()
         copies.append(copy)
+        if k == 0:
+            copy = pltpu.make_async_remote_copy(
+                far.at[half], other.at[half], o_send.at[0], o_recv.at[half],
+                device_id={"rows": (1 - role) * n_y + y, "cls": cls}, device_id_type=MESH,
+            )
+            copy.start()
+            copies.append(copy)
 
     def one_hot(i, carry):
         at = pl.ds(pl.multiple_of(i * LANES, LANES), LANES)
@@ -241,25 +248,60 @@
             far.at[source], far.at[source], f_send.at[d], f_recv.at[source],
             device_id=far_peer(source), device_id_type=MESH,
         ).wait_recv()
-    total = far[0]
-    for k in range(1, n_half):
-        total = total + far[k]
-    lv_t[mine] = -0.3 * total[0] / (total[1] + 1.0)
-
-    for j in near_order:
-        copy = pltpu.make_async_remote_copy(
-            lv_t.at[mine], lv_t.at[mine], g_send.at[j], g_recv.at[j],
-            device_id=near_peer(j), device_id_type=MESH,
-        )
-        copy.start()
-        copies.append(copy)
-    for j in range(1, 2 * n_y):
-        dy, flip = j // 2, j % 2
-        source = lax.rem(y + n_y - dy, n_y) * 2 + (1 - role if flip else role)
-        pltpu.make_async_remote_copy(
-            lv_t.at[source], lv_t.at[source], g_send.at[j], g_recv.at[j],
-            device_id=near_peer(j), device_id_type=MESH,
-        ).wait_recv()
+    def values(parts):
+        total = parts[0]
+        for k in range(1, n_half):
+            total = total + parts[k]
+        return -0.3 * total[0] / (total[1] + 1.0)
+
+    lv_t[mine] = values(far)
+
+    @pl.when(half == 0)
+    def _():
+        for k in range(n_half):
+            pltpu.make_async_remote_copy(
+                other.at[k], other.at[k], o_send.at[0], o_recv.at[k],
+                device_id=core_peer(), device_id_type=MESH,
+            ).wait_recv()
+        lv_t[y * 2 + 1 - role] = values(other)
+        gathers = []
+        for dy in (2, 1, 3):
+            both = lv_t.at[pl.ds(y * 2, 2)]
+            copy = pltpu.make_async_remote_copy(
+                both, both, g_send.at[2 * dy], g_recv.at[2 * dy],
+                device_id=near_peer(2 * dy), device_id_type=MESH,
+            )
+            copy.start()
+            gathers.append(copy)
+        for dy in (1, 3, 2):
+            both = lv_t.at[pl.ds(lax.rem(y + n_y - dy, n_y) * 2, 2)]
+            pltpu.make_async_remote_copy(
+                both, both, g_send.at[2 * dy], g_recv.at[2 * dy],
+                device_id=near_peer(2 * dy), device_id_type=MESH,
+            ).wait_recv()
+        for copy in gathers:
+            copy.wait_send()
+
+    @pl.when(half != 0)
+    def _():
+        gathers = []
+        for j in near_order:
+            copy = pltpu.make_async_remote_copy(
+                lv_t.at[mine], lv_t.at[mine], g_send.at[j], g_recv.at[j],
+                device_id=near_peer(j), device_id_type=MESH,
+            )
+            copy.start()
+            gathers.append(copy)
+        for j in range(1, 2 * n_y):
+            dy, flip = j // 2, j % 2
+            source = lax.rem(y + n_y - dy, n_y) * 2 + (1 - role if flip else role)
+            pltpu.make_async_remote_copy(
+                lv_t.at[source], lv_t.at[source], g_send.at[j], g_recv.at[j],
+                device_id=near_peer(j), device_id_type=MESH,
+            ).wait_recv()
+        for copy in gathers:
+            copy.wait_send()
+
     lv_out[...] = lv_t[...].reshape(width, LEAVES).T
     for copy in copies:
         copy.wait_send()
@@ -316,6 +358,7 @@
                 pltpu.VMEM((2, width, LEAVES), F32),
                 pltpu.VMEM((2 * n_y, 2, piece, LEAVES), F32),
                 pltpu.VMEM((n_z // 2, 2, piece, LEAVES), F32),
+                pltpu.VMEM((n_z // 2, 2, piece, LEAVES), F32),
                 pltpu.VMEM((2 * n_y, piece, LEAVES), F32),
                 pltpu.SemaphoreType.REGULAR((3, 2)),
                 dma((CHUNKS + 2,)),
@@ -326,6 +369,8 @@
                 dma((2 * n_y,)),
                 dma((2 * n_y,)),
                 dma((n_z // 2,)),
+                dma((n_z // 2,)),
+                dma((1,)),
                 dma((n_z // 2,)),
                 dma((2 * n_y,)),
                 dma((2 * n_y,)),

time: 39.1 us -> 40.3 us (1.031)
  the two profiles are of different devices: /device:TPU:8 before, /device:TPU:64 now
where the time goes in v7:
time: 40.3 us; the launch traced here: 40.2 us
  Pallas kernels  39.5 us (98%)
  between operations  0.64 us (2%)
    pallas_call x1, Pallas kernels, per_device(): pl.pallas_call(functools.partial(kernel, n_cls, n_y, n_z), out_shape=(plt...  37.9 us
    pallas_call x1, Pallas kernels, per_device(): pl.pallas_call(update, out_shape=(pltpu.HBM((LEAVES, width), F32), pltpu....  1.61 us

profile of v7, /device:TPU:64, one launch (start us, length us, event | category | flops | bytes accessed | tf_op | source)
XLA Modules:
  0.0 40.2 jit_solution(4929690843353432191)
XLA Ops:
  0.6 37.9 %shard_map.50 = (f32[128,128]{1,0:T(8,128)S(1)}, f32[4096,128]{1,0:T(8,128)S(1)}, bf16[4096,256]{1,0:T(8,128)(2,1)S(1)}) custom-call(f32[4096,128]{1,0:T(8,128)} %x_hbm.1, s32[32,128]{1,0:T(8,128)} %bitcast.2, s32[32,128]{1,0:T(8,128)} %bitcast.3), custom_call_target="tpu_custom_call" | custom-call | tf_op jit(solution)/shard_map/pallas_call | solution.py:342
  38.6 1.6 %shard_map.51 = (f32[128,128]{1,0:T(8,128)}, f32[4096,128]{1,0:T(8,128)}) custom-call(f32[4096,128]{1,0:T(8,128)S(1)} %get-tuple-element.5.x_v, bf16[4096,256]{1,0:T(8,128)(2,1)S(1)} %get-tuple-element.6.onehot, f32[128,128]{1,0:T(8,128)S(1)} %get-tuple-element.7.lv), custom_call_target="tpu_custom_call" | custom-call | tf_op jit(solution)/shard_map/pallas_call | solution.py:386

commit v8 on v6

--- a/solution.py
+++ b/solution.py
@@ -40,7 +40,7 @@
     n_half = n_z // 2
 
     def role_of(of_half, of_odd):
-        return lax.rem(of_odd + of_half // (n_half // 2), 2)
+        return jnp.where(of_half == n_half // 2, 1 - of_odd, of_odd)
 
     role = role_of(half, odd)
     rows, width = x_v.shape

time: 39.1 us -> 38.5 us (0.985)
  Pallas kernels: 38.3 us -> 37.7 us
    pallas_call x1, Pallas kernels: 36.7 us -> 36.1 us  [per_device(): pl.pallas_call(functools.partial(kernel, n_cls, n_y, n_z), out_shape=(plt...]
where the time goes in v8:
time: 38.5 us; the launch traced here: 38.4 us
  Pallas kernels  37.7 us (98%)
  between operations  0.64 us (2%)
    pallas_call x1, Pallas kernels, per_device(): pl.pallas_call(functools.partial(kernel, n_cls, n_y, n_z), out_shape=(plt...  36.1 us
    pallas_call x1, Pallas kernels, per_device(): pl.pallas_call(update, out_shape=(pltpu.HBM((LEAVES, width), F32), pltpu....  1.61 us

profile of v8, /device:TPU:8, one launch (start us, length us, event | category | flops | bytes accessed | tf_op | source)
XLA Modules:
  0.0 38.4 jit_solution(11177420938431297864)
XLA Ops:
  0.6 36.1 %shard_map.50 = (f32[128,128]{1,0:T(8,128)S(1)}, f32[4096,128]{1,0:T(8,128)S(1)}, bf16[4096,256]{1,0:T(8,128)(2,1)S(1)}) custom-call(f32[4096,128]{1,0:T(8,128)} %x_hbm.1, s32[32,128]{1,0:T(8,128)} %bitcast.2, s32[32,128]{1,0:T(8,128)} %bitcast.3), custom_call_target="tpu_custom_call" | custom-call | tf_op jit(solution)/shard_map/pallas_call | solution.py:300
  36.8 1.6 %shard_map.51 = (f32[128,128]{1,0:T(8,128)}, f32[4096,128]{1,0:T(8,128)}) custom-call(f32[4096,128]{1,0:T(8,128)S(1)} %get-tuple-element.5.x_v, bf16[4096,256]{1,0:T(8,128)(2,1)S(1)} %get-tuple-element.6.onehot, f32[128,128]{1,0:T(8,128)S(1)} %get-tuple-element.7.lv), custom_call_target="tpu_custom_call" | custom-call | tf_op jit(solution)/shard_map/pallas_call | solution.py:341

commit v9 on v8

--- a/solution.py
+++ b/solution.py
@@ -83,12 +83,13 @@
 
     barrier = pltpu.get_barrier_semaphore()
     near_order = sorted(range(1, 2 * n_y), key=lambda j: -(min(j // 2, n_y - j // 2) + j % 2))
-    for j in near_order:
+    for j in range(2, 2 * n_y, 2):
         pl.semaphore_signal(barrier, inc=1, device_id=near_peer(j), device_id_type=MESH)
     for d in range(1, n_x):
         pl.semaphore_signal(barrier, inc=1, device_id=x_peer(d), device_id_type=MESH)
     pl.semaphore_signal(barrier, inc=1, device_id=core_peer(), device_id_type=MESH)
-    pl.semaphore_signal(barrier, inc=1, device_id=z_peer(2 * odd - 1), device_id_type=MESH)
+    for d in (-1, 1):
+        pl.semaphore_signal(barrier, inc=1, device_id=z_peer(d), device_id_type=MESH)
 
     def tell(step):
         for side in range(2):
@@ -120,7 +121,7 @@
 
         lax.fori_loop(0, per_chunk, local, 0, unroll=8)
 
-    pl.semaphore_wait(barrier, n_x + 2 * n_y)
+    pl.semaphore_wait(barrier, n_x + n_y + 1)
     swaps = []
     for h in range(PARTS):
         copy = pltpu.make_async_remote_copy(

time: 38.5 us -> 38.2 us (level)
  the two profiles are of different devices: /device:TPU:8 before, /device:TPU:6 now
where the time goes in v9:
time: 38.2 us; the launch traced here: 38 us
  Pallas kernels  37.4 us (98%)
  between operations  0.64 us (2%)
    pallas_call x1, Pallas kernels, per_device(): pl.pallas_call(functools.partial(kernel, n_cls, n_y, n_z), out_shape=(plt...  35.8 us
    pallas_call x1, Pallas kernels, per_device(): pl.pallas_call(update, out_shape=(pltpu.HBM((LEAVES, width), F32), pltpu....  1.6 us

profile of v9, /device:TPU:6, one launch (start us, length us, event | category | flops | bytes accessed | tf_op | source)
XLA Modules:
  0.0 38.0 jit_solution(4494427199843685314)
XLA Ops:
  0.6 35.8 %shard_map.50 = (f32[128,128]{1,0:T(8,128)S(1)}, f32[4096,128]{1,0:T(8,128)S(1)}, bf16[4096,256]{1,0:T(8,128)(2,1)S(1)}) custom-call(f32[4096,128]{1,0:T(8,128)} %x_hbm.1, s32[32,128]{1,0:T(8,128)} %bitcast.2, s32[32,128]{1,0:T(8,128)} %bitcast.3), custom_call_target="tpu_custom_call" | custom-call | tf_op jit(solution)/shard_map/pallas_call | solution.py:301
  36.4 1.6 %shard_map.51 = (f32[128,128]{1,0:T(8,128)}, f32[4096,128]{1,0:T(8,128)}) custom-call(f32[4096,128]{1,0:T(8,128)S(1)} %get-tuple-element.5.x_v, bf16[4096,256]{1,0:T(8,128)(2,1)S(1)} %get-tuple-element.6.onehot, f32[128,128]{1,0:T(8,128)S(1)} %get-tuple-element.7.lv), custom_call_target="tpu_custom_call" | custom-call | tf_op jit(solution)/shard_map/pallas_call | solution.py:342
